TPU v7x, 32 devices: a whole 2x2x4 slice. The times are simulated.
32 devices in a mesh: tm: 4 (over y, x), freq: 8 (over z, core).
Axes of the slice: x: 2, y: 2, z: 4, core: 2. Of those that a mesh axis runs over, the one named last changes fastest.
Arguments:
- records: bfloat16 [1024, 512, 512], P('freq', 'tm'), may hold values from -4 to 4
- gap_flags: int32 [1024, 16], P('freq', 'tm'), may hold values from -2147483648 to 2147483647
- station_mask: int32 [1024], P('freq'), may hold values 0 or 1
Outputs:
- cross_spectra: float32 [16, 2, 1024, 1024], P('freq', None, 'tm')
All inputs are finite; a program needn't handle non-finite values. No bound on the sum of `station_mask` on one device may be relied on, other than what follows from the above.
Results may differ from a plain program's by a relative error of at most 0.0013.
Values may be sent and summed in bfloat16 or wider, within the bound.
No kernel may reach another device: no remote copies, remote signals or barrier semaphores. Data moves between devices by JAX's collectives and lax.ppermute only.
A program may use at most 128 MiB of HBM per device.

v0:
```python
import math
import jax
import jax.numpy as jnp
from jax import lax
from jax.sharding import PartitionSpec as P

BAND_DEV = 2
FLOOR = 0.25


def transform_table(length, bin_count):
    sample_ids = jnp.arange(length, dtype=jnp.int32)
    bin_ids = jnp.arange(bin_count, dtype=jnp.int32)
    phase_ids = bin_ids[:, None] * sample_ids[None, :] % length
    angles = phase_ids.astype(jnp.float32) * (2.0 * math.pi / length)
    window_taper = 0.5 - 0.5 * jnp.cos(sample_ids.astype(jnp.float32) * (2.0 * math.pi / length))
    factor = window_taper / math.sqrt(length)
    dft_table = jnp.concatenate([jnp.cos(angles) * factor, -jnp.sin(angles) * factor], axis=0)
    return dft_table.astype(jnp.bfloat16)


def unpack_flags(packed_words):
    shifts = jnp.arange(32, dtype=jnp.int32)
    bit_values = jnp.bitwise_and(
        jnp.right_shift(packed_words[:, :, None], shifts[None, None, :]), 1
    )
    return bit_values.reshape(packed_words.shape[0], packed_words.shape[1] * 32)


def whiten(records, band_bins):
    bin_count = band_bins + 4
    dft_table = transform_table(records.shape[-1], bin_count)
    spectrum = jnp.einsum("cl,swl->scw", dft_table, records, preferred_element_type=jnp.float32)
    real_part = spectrum[:, :bin_count]
    imag_part = spectrum[:, bin_count:]
    magnitude = jnp.sqrt(real_part * real_part + imag_part * imag_part)
    smooth = (
        magnitude[:, 0:band_bins]
        + magnitude[:, 1 : band_bins + 1]
        + magnitude[:, 2 : band_bins + 2]
        + magnitude[:, 3 : band_bins + 3]
        + magnitude[:, 4 : band_bins + 4]
    ) / 5.0
    factor = 1.0 / jnp.maximum(smooth, FLOOR)
    whitened = jnp.stack(
        [real_part[:, 2 : band_bins + 2] * factor, imag_part[:, 2 : band_bins + 2] * factor], axis=2
    )
    return whitened.astype(jnp.bfloat16)


def block_terms(left_side, right_side):
    count_rows, bin_count, _, win_count = left_side.shape
    right_rows = right_side.shape[0]
    direct_left = left_side.reshape(count_rows, bin_count, 2 * win_count)
    turned_left = jnp.concatenate([left_side[:, :, 1], -left_side[:, :, 0]], axis=2)
    direct_right = right_side.reshape(right_rows, bin_count, 2 * win_count)
    real_part = jnp.einsum(
        "ifx,jfx->ifj", direct_left, direct_right, preferred_element_type=jnp.float32
    )
    imag_part = jnp.einsum(
        "ifx,jfx->ifj", turned_left, direct_right, preferred_element_type=jnp.float32
    )
    return jnp.stack([real_part, imag_part], axis=2).reshape(count_rows, 2 * bin_count, right_rows)


def local(records, gap_flags, station_mask):
    freq_size = lax.axis_size("freq")
    time_size = lax.axis_size("tm")
    band_bins = BAND_DEV * freq_size
    whitened = whiten(records, band_bins)
    kept_words = gap_flags * station_mask[:, None]
    spectra = lax.all_to_all(whitened, "freq", split_axis=1, concat_axis=0, tiled=True)
    all_words = lax.all_gather(kept_words, "freq", axis=0, tiled=True)
    here_flags = unpack_flags(all_words).astype(jnp.bfloat16)
    masked = spectra * here_flags[:, None, None, :]
    stations = spectra.shape[0]
    row_count = stations // time_size
    row_start = lax.axis_index("tm") * row_count
    every_words = lax.all_gather(all_words, "tm", axis=1, tiled=True)
    every_flags = unpack_flags(every_words).astype(jnp.bfloat16)
    row_flags = lax.dynamic_slice_in_dim(every_flags, row_start, row_count, 0)
    counts = jnp.dot(row_flags, every_flags.T, preferred_element_type=jnp.float32)
    window_part = lax.all_gather(masked, "tm", axis=3, tiled=True)
    left_side = lax.dynamic_slice_in_dim(window_part, row_start, row_count, 0)
    stacks = block_terms(left_side, window_part)
    divisor = jnp.maximum(counts, 1.0)
    result = stacks / divisor[:, None, :]
    return result.reshape(row_count, BAND_DEV, 2, stations).transpose(1, 2, 0, 3)


def solution(mesh):
    placed = (P("freq", "tm", None), P("freq", "tm"), P("freq"))
    return jax.shard_map(
        local, mesh=mesh, in_specs=placed, out_specs=P("freq", None, "tm", None), check_vma=False
    )
```

profile of v0, /device:TPU:0, one launch (start us, length us, event | category | flops | bytes accessed | tf_op | source)
XLA Modules:
  0.0 130.0 jit_solution(13890323300610356222)
XLA Ops:
  6.6 0.2 multiply_convert_fusion.1
  6.8 8.5 %convolution_bitcast_fusion = f32[128,40,128]{2,1,0:T(8,128)S(1)} fusion(bf16[128,128,512]{2,1,0:T(8,128)(2,1)} %param.3, bf16[20,512]{1,0:T(8,128)(2,1)S(1)} %get-tuple-element.10, bf16[20,512]{1,0:T(8,128)(2,1)S(1)} %get-tuple-element.9), kind=kOutput, calls=%fused_computation.5 | convolution fusion | flops 671170560 | bytes 19439616 | tf_op jit(solution)/shard_map/cl,swl->scw/dot_general | solution.py:33
  15.3 0.6 fusion.4
  15.9 0.7 fusion.13
  16.6 0.2 fusion.14
  16.8 0.1 pad_maximum_fusion
  16.9 0.0 copy-start.1
  16.9 0.0 copy-start.2
  16.9 1.2 copy.17
  18.2 6.3 %all-to-all-start = ((bf16[128,16,2,128]{3,0,2,1:T(8,128)(2,1)}), bf16[128,16,2,128]{3,0,2,1:T(8,128)(2,1)S(1)}, u32[]{:S(2)}, u32[]{:S(2)}) async-start(bf16[128,16,2,128]{3,0,2,1:T(8,128)(2,1)} %copy.17), calls=%async_computation | async-start | bytes 2097152 | tf_op jit(solution)/shard_map/all_to_all | solution.py:72
  24.5 0.0 all-gather.3.cloned.1.call-start
  24.6 0.1 shift_right_arithmetic.47
  24.7 0.0 copy-done.1
  24.7 0.0 copy-done.2
  24.7 32.5 %all_gather.9 = s32[1024,4]{0,1:T(4,128)S(1)} all-gather(s32[128,4]{0,1:T(4,128)S(1)} %broadcast_multiply_fusion), channel_id=1, replica_groups=mesh['tm'=4,'freq'=8] {'freq'}, dimensions={0}, use_global_device_ids=true | all-gather | bytes 18432 | tf_op jit(solution)/shard_map/all_gather | solution.py:73
  57.2 0.1 fusion.17
  57.3 0.2 copy.19
  57.5 0.0 all-to-all-done
  57.5 0.1 copy.18
  57.6 1.1 bitcast_multiply_fusion
  58.7 0.0 all-gather.3.cloned.1.call-update
  58.8 0.1 shift_right_arithmetic.53
  58.8 8.2 %all-gather = s32[4,4,1024]{2,1,0:T(4,128)S(1)} all-gather(s32[1,4,1024]{2,1,0:T(4,128)S(1)} %bitcast.60), channel_id=1, replica_groups=mesh['tm'=4,'freq'=8] {'tm'}, dimensions={0}, use_global_device_ids=true | all-gather | bytes 81920 | tf_op jit(solution)/shard_map/all_gather | solution.py:79
  67.1 0.3 fusion.2
  67.4 0.5 convolution_maximum_fusion
  67.9 0.3 copy.22
  68.2 41.3 %all-gather.3.cloned.1.call-done = bf16[1024,2,2,512]{3,0,1,2:T(8,128)(2,1)} async-done(((bf16[1024,2,2,128]{3,0,1,2:T(8,128)(2,1)}), bf16[1024,2,2,512]{3,0,1,2:T(8,128)(2,1)}) %all-gather.3.cloned.1.call-update) | async-done | bytes 4194320 | tf_op jit(solution)/shard_map/all_gather | solution.py:83
  109.5 0.0 copy-start
  109.5 1.4 %dynamic-slice_bitcast_fusion = bf16[2,2,32,8,512]{4,3,2,1,0:T(8,128)(2,1)S(1)} fusion(bf16[1024,2,2,512]{3,0,1,2:T(8,128)(2,1)} %all-gather.3.cloned.1.call-done, s32[]{:T(128)S(6)} %select_n.14), kind=kLoop, calls=%fused_computation.29 | loop fusion | bytes 2097156
  111.0 0.1 copy.25
  111.1 0.9 copy-done
  112.1 0.6 copy.24
  112.7 1.3 %convolution_bitcast_fusion.2 = f32[256,2,1,1024]{0,3,1,2:T(8,128)S(1)} fusion(bf16[1024,2,1024]{2,0,1:T(8,128)(2,1)S(1)} %bitcast.54, bf16[256,2,1024]{2,0,1:T(8,128)(2,1)S(1)} %bitcast.57), kind=kOutput, calls=%fused_computation.7 | convolution fusion | flops 1073741824 | bytes 7340032 | tf_op jit(solution)/shard_map/ifx,jfx->ifj/dot_general | solution.py:57
  114.0 0.1 dynamic-slice_bitcast_fusion.1
  114.1 1.3 %convolution_bitcast_fusion.1 = f32[256,2,1,1024]{0,3,1,2:T(8,128)S(1)} fusion(bf16[1024,2,1024]{2,0,1:T(8,128)(2,1)S(1)} %bitcast.55, bf16[256,2,512]{2,0,1:T(8,128)(2,1)S(1)} %get-tuple-element.8, bf16[256,2,512]{2,0,1:T(8,128)(2,1)S(1)} %get-tuple-element.7), kind=kOutput, calls=%fused_computation.6 | convolution fusion | flops 1075838976 | bytes 7340032 | tf_op jit(solution)/shard_map/ifx,jfx->ifj/dot_general | solution.py:60
  115.5 2.3 %fusion = f32[2,2,256,1024]{2,3,0,1:T(8,128)} fusion(f32[256,2,1,1024]{0,3,1,2:T(8,128)S(1)} %convolution_bitcast_fusion.1, f32[256,2,1,1024]{0,3,1,2:T(8,128)S(1)} %convolution_bitcast_fusion.2, f32[256,1024]{0,1:T(8,128)S(1)} %copy.22), kind=kLoop, calls=%fused_computation.1 | loop fusion | flops 2097152 | bytes 9437184 | tf_op jit(solution)/shard_map/transpose | solution.py:88
  117.8 5.3 %copy.23 = f32[2,2,256,1024]{3,2,1,0:T(8,128)} copy(f32[2,2,256,1024]{2,3,0,1:T(8,128)} %fusion) | data formatting | bytes 8388608 | tf_op jit(solution)/shard_map/transpose | solution.py:88
  (5 shorter events, 0.1 us)
Async XLA Ops:
  16.9 7.8 %copy-start.1 = (s32[128,4]{0,1:T(4,128)S(1)}, s32[128,4]{0,1:T(4,128)}, u32[]{:S(2)}) copy-start(s32[128,4]{0,1:T(4,128)} %param.4) | copy-start | bytes 6148
  16.9 7.7 %copy-start.2 = (s32[128]{0:T(128)S(1)}, s32[128]{0:T(128)}, u32[]{:S(2)}) copy-start(s32[128]{0:T(128)} %param.5) | copy-start | bytes 1540
  18.2 39.3 %all-to-all-start = ((bf16[128,16,2,128]{3,0,2,1:T(8,128)(2,1)}), bf16[128,16,2,128]{3,0,2,1:T(8,128)(2,1)S(1)}, u32[]{:S(2)}, u32[]{:S(2)}) async-start(bf16[128,16,2,128]{3,0,2,1:T(8,128)(2,1)} %copy.17), calls=%async_computation | async-start | bytes 2097152 | tf_op jit(solution)/shard_map/all_to_all | solution.py:72
  24.5 85.0 %all-gather.3.cloned.1.call-start = ((), (), s32[]{:S(2)}) async-start(), calls=%async_computation.1 | async-start | bytes 5242880 | tf_op jit(solution)/shard_map/all_gather | solution.py:83
  109.5 2.5 %copy-start = (bf16[1024,2,2,512]{3,0,1,2:T(8,128)(2,1)S(1)}, bf16[1024,2,2,512]{3,0,1,2:T(8,128)(2,1)}, u32[]{:S(2)}) copy-start(bf16[1024,2,2,512]{3,0,1,2:T(8,128)(2,1)} %all-gather.3.cloned.1.call-done) | copy-start | bytes 12582916
Sparse Core Ops, SparseCore 0:
  58.9 50.6 all-gather.2
where the time goes:
time: 130 us
  waiting for transfers between devices  41.3 us (32%)
  blocking collectives  40.7 us (31%)
  between operations  13.6 us (10%)
  matrix products  11.6 us (9%)
  local copies, waits for them, and re-layouts  10.5 us (8%)
  starting transfers between devices  6.38 us (5%)
  other arithmetic  5.85 us (4%)
    all_gather x1, waiting for transfers between devices, local(): window_part = lax.all_gather(masked, 'tm', axis=3, tiled=True)  41.3 us
    all_gather x1, blocking collectives, local(): all_words = lax.all_gather(kept_words, 'freq', axis=0, tiled=True)  32.5 us
    dot_general x1, matrix products, whiten(): jnp.einsum('cl,swl->scw', dft_table, records, preferred_element_type=jnp....  8.47 us
    all_gather x1, blocking collectives, local(): every_words = lax.all_gather(all_words, 'tm', axis=1, tiled=True)  8.24 us
    all_to_all x1, starting transfers between devices, local(): lax.all_to_all(whitened, 'freq', split_axis=1, concat_axis=0, tiled=True)  6.35 us
    transpose x1, local copies, waits for them, and re-layouts, local(): result.reshape(row_count, BAND_DEV, 2, stations).transpose(1, 2, 0, 3)  5.34 us
  transfers between devices with their start and end apart: 2, of which 1 were waited for; matrix products, arithmetic and copies ran while one was open for 1% of the time, Pallas kernels for 0%

commit v1 on v0

--- a/solution.py
+++ b/solution.py
@@ -70,7 +70,14 @@
     whitened = whiten(records, band_bins)
     kept_words = gap_flags * station_mask[:, None]
     spectra = lax.all_to_all(whitened, "freq", split_axis=1, concat_axis=0, tiled=True)
-    all_words = lax.all_gather(kept_words, "freq", axis=0, tiled=True)
+    ways, here = (lax.axis_size("freq"), lax.axis_index("freq"))
+    all_words, reach = (kept_words, 1)
+    while reach < ways:
+        theirs = lax.ppermute(all_words, "freq", [(d, d ^ reach) for d in range(ways)])
+        mine_first = jnp.concatenate([all_words, theirs], axis=0)
+        theirs_first = jnp.concatenate([theirs, all_words], axis=0)
+        all_words = jnp.where(here & reach == 0, mine_first, theirs_first)
+        reach = 2 * reach
     here_flags = unpack_flags(all_words).astype(jnp.bfloat16)
     masked = spectra * here_flags[:, None, None, :]
     stations = spectra.shape[0]

time: 130 us -> 125 us (0.962)
  blocking collectives: 40.7 us -> 8.24 us
  waiting for transfers between devices: 41.3 us -> 62.1 us
  starting transfers between devices: 6.38 us -> 13.1 us
    all_gather x1 -> x0, blocking collectives: 32.5 us -> none  [local(): all_words = lax.all_gather(kept_words, 'freq', axis=0, tiled=True)]
    ppermute x0 -> x3, waiting for transfers between devices: none -> 20 us  [local(): lax.ppermute(all_words, 'freq', [(d, d ^ reach) for d in range(ways)])]
    ppermute x0 -> x3, starting transfers between devices: none -> 6.69 us  [local(): lax.ppermute(all_words, 'freq', [(d, d ^ reach) for d in range(ways)])]
  transfers between devices with their start and end apart: 2 -> 5, of which waited for: 1 -> 4; matrix products, arithmetic and copies ran while one was open for 1% -> 1% of each run, Pallas kernels for 0% -> 0%
where the time goes in v1:
time: 125 us
  waiting for transfers between devices  62.1 us (50%)
  between operations  13.6 us (11%)
  starting transfers between devices  13.1 us (10%)
  matrix products  11.6 us (9%)
  local copies, waits for them, and re-layouts  10.5 us (8%)
  blocking collectives  8.24 us (7%)
  other arithmetic  5.86 us (5%)
    all_gather x1, waiting for transfers between devices, local(): window_part = lax.all_gather(masked, 'tm', axis=3, tiled=True)  42.1 us
    ppermute x3, waiting for transfers between devices, local(): lax.ppermute(all_words, 'freq', [(d, d ^ reach) for d in range(ways)])  20 us
    dot_general x1, matrix products, whiten(): jnp.einsum('cl,swl->scw', dft_table, records, preferred_element_type=jnp....  8.47 us
    all_gather x1, blocking collectives, local(): every_words = lax.all_gather(all_words, 'tm', axis=1, tiled=True)  8.24 us
    ppermute x3, starting transfers between devices, local(): lax.ppermute(all_words, 'freq', [(d, d ^ reach) for d in range(ways)])  6.69 us
    all_to_all x1, starting transfers between devices, local(): lax.all_to_all(whitened, 'freq', split_axis=1, concat_axis=0, tiled=True)  6.35 us
    transpose x1, local copies, waits for them, and re-layouts, local(): result.reshape(row_count, BAND_DEV, 2, stations).transpose(1, 2, 0, 3)  5.34 us
  transfers between devices with their start and end apart: 5, of which 4 were waited for; matrix products, arithmetic and copies ran while one was open for 1% of the time, Pallas kernels for 0%

profile of v1, /device:TPU:0, one launch (start us, length us, event | category | flops | bytes accessed | tf_op | source)
XLA Modules:
  0.0 125.0 jit_solution(11087243314948961774)
XLA Ops:
  6.6 0.2 multiply_convert_fusion.1
  6.8 8.5 %convolution_bitcast_fusion = f32[128,40,128]{2,1,0:T(8,128)S(1)} fusion(bf16[128,128,512]{2,1,0:T(8,128)(2,1)} %param.3, bf16[20,512]{1,0:T(8,128)(2,1)S(1)} %get-tuple-element.10, bf16[20,512]{1,0:T(8,128)(2,1)S(1)} %get-tuple-element.9), kind=kOutput, calls=%fused_computation.5 | convolution fusion | flops 671170560 | bytes 19439616 | tf_op jit(solution)/shard_map/cl,swl->scw/dot_general | solution.py:33
  15.3 0.6 fusion.4
  15.9 0.7 fusion.13
  16.6 0.2 fusion.14
  16.8 0.1 pad_maximum_fusion
  16.9 0.0 copy-start.1
  16.9 0.0 copy-start.2
  16.9 1.2 copy.17
  18.2 6.3 %all-to-all-start = ((bf16[128,16,2,128]{3,0,2,1:T(8,128)(2,1)}), bf16[128,16,2,128]{3,0,2,1:T(8,128)(2,1)S(1)}, u32[]{:S(2)}, u32[]{:S(2)}) async-start(bf16[128,16,2,128]{3,0,2,1:T(8,128)(2,1)} %copy.17), calls=%async_computation | async-start | bytes 2097152 | tf_op jit(solution)/shard_map/all_to_all | solution.py:72
  24.5 0.0 all-gather.3.cloned.1.call-start
  24.6 0.0 copy-done.1
  24.6 0.0 copy-done.2
  24.6 0.5 collective-permute-start
  25.1 1.0 collective-permute-done
  26.1 1.7 %collective-permute-start.1 = (s32[256,4]{0,1:T(4,128)S(1)}, s32[256,4]{0,1:T(4,128)S(1)}, u32[]{:S(2)}, u32[]{:S(2)}) collective-permute-start(s32[256,4]{0,1:T(4,128)S(1)} %add_select_fusion.3), channel_id=1, source_target_pairs={{0,2},{1,3},{2,0},{3,1},{4,6},{5,7},{6,4},{7,5},{8,10},{9,11},{10,... | collective-permute-start | bytes 12296 | tf_op jit(solution)/shard_map/ppermute | solution.py:76
  27.8 14.9 %collective-permute-done.1 = s32[256,4]{0,1:T(4,128)S(1)} collective-permute-done((s32[256,4]{0,1:T(4,128)S(1)}, s32[256,4]{0,1:T(4,128)S(1)}, u32[]{:S(2)}, u32[]{:S(2)}) %collective-permute-start.1) | collective-permute-done | bytes 4128 | tf_op jit(solution)/shard_map/ppermute | solution.py:76
  42.7 4.4 %collective-permute-start.2 = (s32[512,4]{0,1:T(4,128)S(1)}, s32[512,4]{0,1:T(4,128)S(1)}, u32[]{:S(2)}, u32[]{:S(2)}) collective-permute-start(s32[512,4]{0,1:T(4,128)S(1)} %add_select_fusion.2), channel_id=1, source_target_pairs={{0,4},{1,5},{2,6},{3,7},{4,0},{5,1},{6,2},{7,3},{8,12},{9,13},{10,... | collective-permute-start | bytes 24584 | tf_op jit(solution)/shard_map/ppermute | solution.py:76
  47.1 0.1 shift_right_arithmetic.47
  47.2 4.2 %collective-permute-done.2 = s32[512,4]{0,1:T(4,128)S(1)} collective-permute-done((s32[512,4]{0,1:T(4,128)S(1)}, s32[512,4]{0,1:T(4,128)S(1)}, u32[]{:S(2)}, u32[]{:S(2)}) %collective-permute-start.2) | collective-permute-done | bytes 8224 | tf_op jit(solution)/shard_map/ppermute | solution.py:76
  51.4 0.1 fusion.17
  51.6 0.2 copy.19
  51.8 0.0 all-to-all-done
  51.8 0.1 copy.18
  51.8 1.1 bitcast_multiply_fusion
  53.0 0.0 all-gather.3.cloned.1.call-update
  53.0 0.1 shift_right_arithmetic.53
  53.1 8.2 %all-gather = s32[4,4,1024]{2,1,0:T(4,128)S(1)} all-gather(s32[1,4,1024]{2,1,0:T(4,128)S(1)} %bitcast.60), channel_id=1, replica_groups=mesh['tm'=4,'freq'=8] {'tm'}, dimensions={0}, use_global_device_ids=true | all-gather | bytes 81920 | tf_op jit(solution)/shard_map/all_gather | solution.py:86
  61.4 0.3 fusion.2
  61.7 0.5 convolution_maximum_fusion
  62.2 0.3 copy.22
  62.5 42.1 %all-gather.3.cloned.1.call-done = bf16[1024,2,2,512]{3,0,1,2:T(8,128)(2,1)} async-done(((bf16[1024,2,2,128]{3,0,1,2:T(8,128)(2,1)}), bf16[1024,2,2,512]{3,0,1,2:T(8,128)(2,1)}) %all-gather.3.cloned.1.call-update) | async-done | bytes 4194320 | tf_op jit(solution)/shard_map/all_gather | solution.py:90
  104.6 0.0 copy-start
  104.6 1.4 %dynamic-slice_bitcast_fusion = bf16[2,2,32,8,512]{4,3,2,1,0:T(8,128)(2,1)S(1)} fusion(bf16[1024,2,2,512]{3,0,1,2:T(8,128)(2,1)} %all-gather.3.cloned.1.call-done, s32[]{:T(128)S(6)} %select_n.51), kind=kLoop, calls=%fused_computation.29 | loop fusion | bytes 2097156
  106.0 0.1 copy.25
  106.2 0.9 copy-done
  107.1 0.6 copy.24
  107.7 1.3 %convolution_bitcast_fusion.2 = f32[256,2,1,1024]{0,3,1,2:T(8,128)S(1)} fusion(bf16[1024,2,1024]{2,0,1:T(8,128)(2,1)S(1)} %bitcast.54, bf16[256,2,1024]{2,0,1:T(8,128)(2,1)S(1)} %bitcast.57), kind=kOutput, calls=%fused_computation.7 | convolution fusion | flops 1073741824 | bytes 7340032 | tf_op jit(solution)/shard_map/ifx,jfx->ifj/dot_general | solution.py:57
  109.0 0.1 dynamic-slice_bitcast_fusion.1
  109.2 1.3 %convolution_bitcast_fusion.1 = f32[256,2,1,1024]{0,3,1,2:T(8,128)S(1)} fusion(bf16[1024,2,1024]{2,0,1:T(8,128)(2,1)S(1)} %bitcast.55, bf16[256,2,512]{2,0,1:T(8,128)(2,1)S(1)} %get-tuple-element.8, bf16[256,2,512]{2,0,1:T(8,128)(2,1)S(1)} %get-tuple-element.7), kind=kOutput, calls=%fused_computation.6 | convolution fusion | flops 1075838976 | bytes 7340032 | tf_op jit(solution)/shard_map/ifx,jfx->ifj/dot_general | solution.py:60
  110.5 2.3 %fusion = f32[2,2,256,1024]{2,3,0,1:T(8,128)} fusion(f32[256,2,1,1024]{0,3,1,2:T(8,128)S(1)} %convolution_bitcast_fusion.1, f32[256,2,1,1024]{0,3,1,2:T(8,128)S(1)} %convolution_bitcast_fusion.2, f32[256,1024]{0,1:T(8,128)S(1)} %copy.22), kind=kLoop, calls=%fused_computation.1 | loop fusion | flops 2097152 | bytes 9437184 | tf_op jit(solution)/shard_map/transpose | solution.py:95
  112.8 5.3 %copy.23 = f32[2,2,256,1024]{3,2,1,0:T(8,128)} copy(f32[2,2,256,1024]{2,3,0,1:T(8,128)} %fusion) | data formatting | bytes 8388608 | tf_op jit(solution)/shard_map/transpose | solution.py:95
  (8 shorter events, 0.1 us)
Async XLA Ops:
  16.9 7.7 %copy-start.1 = (s32[128,4]{0,1:T(4,128)S(1)}, s32[128,4]{0,1:T(4,128)}, u32[]{:S(2)}) copy-start(s32[128,4]{0,1:T(4,128)} %param.4) | copy-start | bytes 6148
  16.9 7.7 %copy-start.2 = (s32[128]{0:T(128)S(1)}, s32[128]{0:T(128)}, u32[]{:S(2)}) copy-start(s32[128]{0:T(128)} %param.5) | copy-start | bytes 1540
  18.2 33.6 %all-to-all-start = ((bf16[128,16,2,128]{3,0,2,1:T(8,128)(2,1)}), bf16[128,16,2,128]{3,0,2,1:T(8,128)(2,1)S(1)}, u32[]{:S(2)}, u32[]{:S(2)}) async-start(bf16[128,16,2,128]{3,0,2,1:T(8,128)(2,1)} %copy.17), calls=%async_computation | async-start | bytes 2097152 | tf_op jit(solution)/shard_map/all_to_all | solution.py:72
  24.5 80.0 %all-gather.3.cloned.1.call-start = ((), (), s32[]{:S(2)}) async-start(), calls=%async_computation.1 | async-start | bytes 5242880 | tf_op jit(solution)/shard_map/all_gather | solution.py:90
  24.6 1.5 %collective-permute-start = (s32[128,4]{0,1:T(4,128)S(1)}, s32[128,4]{0,1:T(4,128)S(1)}, u32[]{:S(2)}, u32[]{:S(2)}) collective-permute-start(s32[128,4]{0,1:T(4,128)S(1)} %broadcast_multiply_fusion), channel_id=1, source_target_pairs={{0,1},{1,0},{2,3},{3,2},{4,5},{5,4},{6,7},{7,6},{8,9},{9,8},{10,11... | collective-permute-start | bytes 6152 | tf_op jit(solution)/shard_map/ppermute | solution.py:76
  26.1 16.6 %collective-permute-start.1 = (s32[256,4]{0,1:T(4,128)S(1)}, s32[256,4]{0,1:T(4,128)S(1)}, u32[]{:S(2)}, u32[]{:S(2)}) collective-permute-start(s32[256,4]{0,1:T(4,128)S(1)} %add_select_fusion.3), channel_id=1, source_target_pairs={{0,2},{1,3},{2,0},{3,1},{4,6},{5,7},{6,4},{7,5},{8,10},{9,11},{10,... | collective-permute-start | bytes 12296 | tf_op jit(solution)/shard_map/ppermute | solution.py:76
  42.7 8.8 %collective-permute-start.2 = (s32[512,4]{0,1:T(4,128)S(1)}, s32[512,4]{0,1:T(4,128)S(1)}, u32[]{:S(2)}, u32[]{:S(2)}) collective-permute-start(s32[512,4]{0,1:T(4,128)S(1)} %add_select_fusion.2), channel_id=1, source_target_pairs={{0,4},{1,5},{2,6},{3,7},{4,0},{5,1},{6,2},{7,3},{8,12},{9,13},{10,... | collective-permute-start | bytes 24584 | tf_op jit(solution)/shard_map/ppermute | solution.py:76
  104.6 2.5 %copy-start = (bf16[1024,2,2,512]{3,0,1,2:T(8,128)(2,1)S(1)}, bf16[1024,2,2,512]{3,0,1,2:T(8,128)(2,1)}, u32[]{:S(2)}) copy-start(bf16[1024,2,2,512]{3,0,1,2:T(8,128)(2,1)} %all-gather.3.cloned.1.call-done) | copy-start | bytes 12582916
Sparse Core Ops, SparseCore 0:
  53.1 51.4 all-gather.2
